TPU v7x, 32 devices: a whole 2x2x4 slice. The times are simulated.
32 devices in a mesh: fsdp: 4 (over x, core), ctx: 4 (over z), tp: 2 (over y).
Axes of the slice: x: 2, y: 2, z: 4, core: 2. Of those that a mesh axis runs over, the one named last changes fastest.
Arguments:
- layer_input: bfloat16 [4096, 2048], P(('fsdp', 'ctx', 'tp')), may hold values from -6 to 6
- cotangent: bfloat16 [4096, 2048], P(('fsdp', 'ctx', 'tp')), may hold values from -6 to 6
- lengths: int32 [4, 2], P('fsdp'), may hold values from 0 to 1024, as said below
- attn_norm: bfloat16 [2048], replicated, may hold values from 0.5 to 1.5
- query_norm_gain: bfloat16 [128], replicated, may hold values from 0.25 to 1.75
- k_norm: bfloat16 [128], replicated, may hold values from 0.25 to 1.75
- w_query: bfloat16 [2048, 2048], P('fsdp', 'tp'), may hold values from -0.125 to 0.125
- key_weight: bfloat16 [2048, 1024], P('fsdp', 'tp'), may hold values from -0.125 to 0.125
- value_weight: bfloat16 [2048, 1024], P('fsdp', 'tp'), may hold values from -0.125 to 0.125
- w_out_gate: bfloat16 [2048, 2048], P('fsdp', 'tp'), may hold values from -0.125 to 0.125
- w_output: bfloat16 [2048, 2048], P(('tp', 'fsdp')), may hold values from -2 to 2
- ffn_norm: bfloat16 [2048], replicated, may hold values from 0.5 to 1.5
- w_gate: bfloat16 [2048, 6144], P('fsdp', 'tp'), may hold values from -0.125 to 0.125
- w_up: bfloat16 [2048, 6144], P('fsdp', 'tp'), may hold values from -0.125 to 0.125
- w_down: bfloat16 [6144, 2048], P(('tp', 'fsdp')), may hold values from -0.078125 to 0.078125
Outputs:
- layer_output: bfloat16 [4096, 2048], P(('fsdp', 'ctx', 'tp'))
- input_grad: bfloat16 [4096, 2048], P(('fsdp', 'ctx', 'tp'))
- grad_attn_norm: float32 [2048], replicated
- grad_q_norm: float32 [128], replicated
- grad_k_norm: float32 [128], replicated
- grad_w_query: float32 [2048, 2048], P('fsdp', 'tp')
- grad_w_key: float32 [2048, 1024], P('fsdp', 'tp')
- grad_w_value: float32 [2048, 1024], P('fsdp', 'tp')
- grad_w_out_gate: float32 [2048, 2048], P('fsdp', 'tp')
- grad_w_output: float32 [2048, 2048], P(('tp', 'fsdp'))
- grad_ffn_norm: float32 [2048], replicated
- grad_w_gate: float32 [2048, 6144], P('fsdp', 'tp')
- grad_w_up: float32 [2048, 6144], P('fsdp', 'tp')
- grad_w_down: float32 [6144, 2048], P(('tp', 'fsdp'))
Inputs may be any that keep to these rules, and one draw needn't show every extreme that they name: `lengths`: per packed row the first count is at least 512 and the two counts add up to at most 1024; some row holds a single sequence of 1024 tokens.
All inputs are finite; a program needn't handle non-finite values.
Results may differ from a plain program's by a relative error of at most 0.024.
Values may be sent and summed in bfloat16 or wider, within the bound.
No kernel may reach another device: no remote copies, remote signals or barrier semaphores. Data moves between devices by JAX's collectives and lax.ppermute only.
A program may use at most 448 MiB of HBM per device.

v0:
```python
import jax
import jax.numpy as jnp
from jax import lax
from jax.sharding import PartitionSpec as P

HEAD_SIZE = 128
EPSILON = 1e-06
ROPE_BASE = 1000000.0
NEG_FILL = -1e30


def as_sent(value):

    def short(part):
        return part.astype(jnp.bfloat16) if part.dtype == jnp.float32 else part

    return jax.tree.map(short, value)


def apply_rms_norm(values, gain_vec):
    return (
        values * lax.rsqrt(jnp.mean(values * values, axis=-1, keepdims=True) + EPSILON) * gain_vec
    )


def norm_back(values, gain_vec, grad_in):
    row_scale = lax.rsqrt(jnp.mean(values * values, axis=-1, keepdims=True) + EPSILON)
    unit_rows = values * row_scale
    scaled = grad_in * gain_vec
    back_rows = row_scale * (
        scaled - unit_rows * jnp.mean(scaled * unit_rows, axis=-1, keepdims=True)
    )
    gain_grad = jnp.sum((grad_in * unit_rows).reshape(-1, values.shape[-1]), axis=0)
    return (back_rows, gain_grad)


def apply_rotary(values, token_position, direction):
    half_size = values.shape[-1] // 2
    frequency = jnp.power(ROPE_BASE, -jnp.arange(half_size, dtype=jnp.float32) / half_size)
    angle = token_position.astype(jnp.float32)[:, None] * frequency[None, :]
    cosine = jnp.cos(angle)[:, None, :]
    sine = direction * jnp.sin(angle)[:, None, :]
    first_half = values[..., :half_size]
    second_half = values[..., half_size:]
    return jnp.concatenate(
        [first_half * cosine - second_half * sine, second_half * cosine + first_half * sine],
        axis=-1,
    )


def segment_of(slot_ids, lengths):
    first_len = lengths[0, 0]
    second_len = lengths[0, 1]
    return jnp.where(slot_ids < first_len, 0, jnp.where(slot_ids < first_len + second_len, 1, 2))


def position_of(slot_ids, segment, lengths):
    seg_begin = jnp.where(
        segment == 0, 0, jnp.where(segment == 1, lengths[0, 0], lengths[0, 0] + lengths[0, 1])
    )
    return slot_ids - seg_begin


def to_block(local_part):
    return lax.all_gather(local_part, "tp", axis=0, tiled=True)


def to_share(partial_rows):
    return lax.psum_scatter(
        partial_rows.astype(jnp.bfloat16), "tp", scatter_dimension=0, tiled=True
    ).astype(jnp.float32)


def fold_product(left_rows, weight_set):
    pieces = jax.tree.map(
        lambda a: lax.all_gather(a, "fsdp", axis=0, tiled=True), as_sent(weight_set)
    )
    return tuple(
        (
            jnp.dot(left_rows, weight_part, preferred_element_type=jnp.float32)
            for weight_part in pieces
        )
    )


def back_product(grad_rows, weight_set):
    pieces = jax.tree.map(
        lambda a: lax.all_gather(a, "fsdp", axis=0, tiled=True), as_sent(weight_set)
    )
    result = lax.dot_general(
        grad_rows[0], pieces[0], (((1,), (1,)), ((), ())), preferred_element_type=jnp.float32
    )
    for grad_part, weight_part in zip(grad_rows[1:], pieces[1:]):
        result = result + lax.dot_general(
            grad_part, weight_part, (((1,), (1,)), ((), ())), preferred_element_type=jnp.float32
        )
    return result


def weight_grads(left_rows, grad_rows):
    widths = [grad_part.shape[1] for grad_part in grad_rows]
    shared = lax.psum_scatter(
        jnp.concatenate(
            [
                lax.dot_general(
                    left_rows,
                    grad_part,
                    (((0,), (0,)), ((), ())),
                    preferred_element_type=jnp.float32,
                )
                for grad_part in grad_rows
            ],
            axis=1,
        ).astype(jnp.bfloat16),
        "fsdp",
        scatter_dimension=0,
        tiled=True,
    )
    summed = lax.psum(shared, "ctx").astype(jnp.float32)
    pieces = []
    offset = 0
    for column_width in widths:
        pieces.append(summed[:, offset : offset + column_width])
        offset = offset + column_width
    return tuple(pieces)


def body(
    layer_input,
    cotangent,
    lengths,
    attn_norm,
    query_norm_gain,
    k_norm,
    w_query,
    key_weight,
    value_weight,
    w_out_gate,
    w_output,
    ffn_norm,
    w_gate,
    w_up,
    w_down,
):
    local_rows = layer_input.shape[0]
    block_rows = local_rows * lax.axis_size("tp")
    query_heads = w_query.shape[1] // HEAD_SIZE
    kv_heads = key_weight.shape[1] // HEAD_SIZE
    groups = query_heads // kv_heads
    score_scale = HEAD_SIZE ** (-0.5)
    block_first = lax.axis_index("ctx") * block_rows
    own_slots = (
        block_first + lax.axis_index("tp") * local_rows + jnp.arange(local_rows, dtype=jnp.int32)
    )
    own_valid = (segment_of(own_slots, lengths) < 2).astype(jnp.float32)[:, None]
    query_slots = block_first + jnp.arange(block_rows, dtype=jnp.int32)
    query_segment = segment_of(query_slots, lengths)
    query_position = position_of(query_slots, query_segment, lengths)
    inputs = layer_input.astype(jnp.float32)
    gain_one = attn_norm.astype(jnp.float32)
    gain_two = ffn_norm.astype(jnp.float32)
    query_gain = query_norm_gain.astype(jnp.float32)
    key_gain = k_norm.astype(jnp.float32)
    first_normed = to_block(apply_rms_norm(inputs, gain_one).astype(jnp.bfloat16))
    query_rows, key_projected, value_proj, gate_logits = fold_product(
        first_normed, (w_query, key_weight, value_weight, w_out_gate)
    )
    query_heads_raw = query_rows.reshape(block_rows, query_heads, HEAD_SIZE)
    key_heads_raw = key_projected.reshape(block_rows, kv_heads, HEAD_SIZE)
    query_rotated = apply_rotary(
        apply_rms_norm(query_heads_raw, query_gain), query_position, 1.0
    ).astype(jnp.bfloat16)
    key_rot = apply_rotary(apply_rms_norm(key_heads_raw, key_gain), query_position, 1.0).astype(
        jnp.bfloat16
    )
    query_grouped = query_rotated.reshape(block_rows, kv_heads, groups, HEAD_SIZE)
    key_flat = key_rot.reshape(block_rows, kv_heads * HEAD_SIZE)
    value_reduced = value_proj.astype(jnp.bfloat16)

    def key_mask(piece_rows):
        key_slots = jnp.arange(piece_rows, dtype=jnp.int32)
        key_segment = segment_of(key_slots, lengths)
        return (query_segment[:, None] == key_segment[None, :]) & (
            key_slots[None, :] <= query_slots[:, None]
        )

    head_shape = (kv_heads, groups, block_rows)
    running_top = jnp.full(head_shape + (1,), NEG_FILL, jnp.float32)
    key_piece = lax.all_gather(key_flat, "ctx", axis=0, tiled=True)
    value_piece = lax.all_gather(value_reduced, "ctx", axis=0, tiled=True)
    piece_rows = key_piece.shape[0]
    allowed = key_mask(piece_rows)
    raw_scores = jnp.einsum(
        "qhgd,khd->hgqk",
        query_grouped,
        key_piece.reshape(piece_rows, kv_heads, HEAD_SIZE),
        preferred_element_type=jnp.float32,
    )
    scores = jnp.where(allowed, raw_scores * score_scale, NEG_FILL)
    new_top = jnp.maximum(running_top, jnp.max(scores, axis=-1, keepdims=True))
    weights = jnp.where(allowed, jnp.exp(scores - new_top), 0.0)
    running_total = jnp.sum(weights, axis=-1, keepdims=True)
    mixed_sum = jnp.einsum(
        "hgqk,khd->hgqd",
        weights.astype(jnp.bfloat16),
        value_piece.reshape(piece_rows, kv_heads, HEAD_SIZE),
        preferred_element_type=jnp.float32,
    )
    mixed_sum, running_top, running_total = (mixed_sum, new_top, running_total)
    log_total = running_top + jnp.log(running_total)
    attended = jnp.transpose(mixed_sum / running_total, (2, 0, 1, 3))
    attended_rows = attended.reshape(block_rows, query_heads * HEAD_SIZE)
    gate_sig = jax.nn.sigmoid(gate_logits)
    gated_mix = (attended_rows * gate_sig).astype(jnp.bfloat16)
    attn_share = to_share(fold_product(gated_mix, (w_output,))[0])
    hidden_in = inputs + own_valid * attn_share
    normed_two = to_block(apply_rms_norm(hidden_in, gain_two).astype(jnp.bfloat16))
    gate_pre, up_pre = fold_product(normed_two, (w_gate, w_up))
    gate_sigmoid = jax.nn.sigmoid(gate_pre)
    activated = gate_pre * gate_sigmoid
    hidden_act = (activated * up_pre).astype(jnp.bfloat16)
    ffn_share = to_share(fold_product(hidden_act, (w_down,))[0])
    layer_output = (hidden_in + own_valid * ffn_share).astype(jnp.bfloat16)
    out_grad = cotangent.astype(jnp.float32) * own_valid
    ffn_grad = to_block(out_grad.astype(jnp.bfloat16))
    hidden_grad = back_product((ffn_grad,), (w_down,))
    grad_w_down = weight_grads(hidden_act, (ffn_grad,))[0]
    gate_grad = (
        hidden_grad * up_pre * gate_sigmoid * (1.0 + gate_pre * (1.0 - gate_sigmoid))
    ).astype(jnp.bfloat16)
    up_grad = (hidden_grad * activated).astype(jnp.bfloat16)
    normed_two_grad = to_share(back_product((gate_grad, up_grad), (w_gate, w_up)))
    grad_w_gate, grad_w_up = weight_grads(normed_two, (gate_grad, up_grad))
    back_two, gain_two_grad = norm_back(hidden_in, gain_two, normed_two_grad)
    hidden_total_grad = out_grad + back_two
    attn_grad = to_block((own_valid * hidden_total_grad).astype(jnp.bfloat16))
    gated_grad = back_product((attn_grad,), (w_output,))
    grad_w_output = weight_grads(gated_mix, (attn_grad,))[0]
    mixed_grad = (gated_grad * gate_sig).astype(jnp.bfloat16)
    gate_logit_grad = (gated_grad * attended_rows * gate_sig * (1.0 - gate_sig)).astype(
        jnp.bfloat16
    )
    mixed_grad_heads = mixed_grad.reshape(block_rows, kv_heads, groups, HEAD_SIZE)
    delta_rows = jnp.transpose(
        jnp.sum(mixed_grad_heads.astype(jnp.float32) * attended, axis=-1), (1, 2, 0)
    )[..., None]
    key_piece = lax.all_gather(key_flat, "ctx", axis=0, tiled=True)
    value_piece = lax.all_gather(value_reduced, "ctx", axis=0, tiled=True)
    piece_rows = key_piece.shape[0]
    key_view = key_piece.reshape(piece_rows, kv_heads, HEAD_SIZE)
    value_view = value_piece.reshape(piece_rows, kv_heads, HEAD_SIZE)
    allowed = key_mask(piece_rows)
    raw_scores = jnp.einsum(
        "qhgd,khd->hgqk", query_grouped, key_view, preferred_element_type=jnp.float32
    )
    soft_vals = jnp.where(allowed, jnp.exp(raw_scores * score_scale - log_total), 0.0)
    prob_grad = jnp.einsum(
        "qhgd,khd->hgqk", mixed_grad_heads, value_view, preferred_element_type=jnp.float32
    )
    score_grad = (soft_vals * (prob_grad - delta_rows) * score_scale).astype(jnp.bfloat16)
    query_acc = jnp.einsum(
        "hgqk,khd->qhgd", score_grad, key_view, preferred_element_type=jnp.float32
    )
    key_part = jnp.einsum(
        "hgqk,qhgd->khd", score_grad, query_grouped, preferred_element_type=jnp.float32
    ).reshape(piece_rows, kv_heads * HEAD_SIZE)
    value_part = jnp.einsum(
        "hgqk,qhgd->khd",
        soft_vals.astype(jnp.bfloat16),
        mixed_grad_heads,
        preferred_element_type=jnp.float32,
    ).reshape(piece_rows, kv_heads * HEAD_SIZE)
    kv_acc = jnp.concatenate([key_part, value_part], axis=1)
    query_acc, kv_acc = (query_acc, kv_acc)
    kv_own = lax.psum_scatter(
        kv_acc.astype(jnp.bfloat16), "ctx", scatter_dimension=0, tiled=True
    ).astype(jnp.float32)
    key_rot_grad = kv_own[:, : kv_heads * HEAD_SIZE].reshape(block_rows, kv_heads, HEAD_SIZE)
    value_grad = kv_own[:, kv_heads * HEAD_SIZE :].astype(jnp.bfloat16)
    key_back, key_gain_grad = norm_back(
        key_heads_raw, key_gain, apply_rotary(key_rot_grad, query_position, -1.0)
    )
    query_back, query_gain_grad = norm_back(
        query_heads_raw,
        query_gain,
        apply_rotary(query_acc.reshape(block_rows, query_heads, HEAD_SIZE), query_position, -1.0),
    )
    query_grad = query_back.reshape(block_rows, query_heads * HEAD_SIZE).astype(jnp.bfloat16)
    key_grad = key_back.reshape(block_rows, kv_heads * HEAD_SIZE).astype(jnp.bfloat16)
    attn_in_grads = (query_grad, key_grad, value_grad, gate_logit_grad)
    normed_one_grad = to_share(
        back_product(attn_in_grads, (w_query, key_weight, value_weight, w_out_gate))
    )
    grad_w_query, grad_w_key, grad_w_value, grad_w_out_gate = weight_grads(
        first_normed, attn_in_grads
    )
    back_one, gain_one_grad = norm_back(inputs, gain_one, normed_one_grad)
    input_grad = (hidden_total_grad + back_one).astype(jnp.bfloat16)
    gain_totals = lax.psum(
        (gain_one_grad, query_gain_grad, key_gain_grad, gain_two_grad), ("fsdp", "ctx", "tp")
    )
    return (
        layer_output,
        input_grad,
        gain_totals[0],
        gain_totals[1],
        gain_totals[2],
        grad_w_query,
        grad_w_key,
        grad_w_value,
        grad_w_out_gate,
        grad_w_output,
        gain_totals[3],
        grad_w_gate,
        grad_w_up,
        grad_w_down,
    )


def solution(mesh):
    return jax.shard_map(
        body,
        mesh=mesh,
        in_specs=(
            P(("fsdp", "ctx", "tp"), None),
            P(("fsdp", "ctx", "tp"), None),
            P("fsdp", None),
            P(),
            P(),
            P(),
            P("fsdp", "tp"),
            P("fsdp", "tp"),
            P("fsdp", "tp"),
            P("fsdp", "tp"),
            P(("tp", "fsdp"), None),
            P(),
            P("fsdp", "tp"),
            P("fsdp", "tp"),
            P(("tp", "fsdp"), None),
        ),
        out_specs=(
            P(("fsdp", "ctx", "tp"), None),
            P(("fsdp", "ctx", "tp"), None),
            P(),
            P(),
            P(),
            P("fsdp", "tp"),
            P("fsdp", "tp"),
            P("fsdp", "tp"),
            P("fsdp", "tp"),
            P(("tp", "fsdp"), None),
            P(),
            P("fsdp", "tp"),
            P("fsdp", "tp"),
            P(("tp", "fsdp"), None),
        ),
        check_vma=False,
    )
```

profile of v0, /device:TPU:0, one launch (start us, length us, event | category | flops | bytes accessed | tf_op | source)
XLA Modules:
  0.0 1699.3 jit_solution(15141842273888128146)
XLA Ops:
  12.8 22.6 %all-gather.15.cloned.1.call-done = bf16[256,2048]{1,0:T(8,128)(2,1)} async-done(((bf16[128,2048]{1,0:T(8,128)(2,1)}), bf16[256,2048]{1,0:T(8,128)(2,1)}) %all-gather.15.cloned.1.call-update) | async-done | bytes 1048592 | tf_op jit(solution)/shard_map/all_gather | solution.py:65
  35.4 24.1 %all-gather.23.cloned.1.call-done = bf16[2048,512]{1,0:T(8,128)(2,1)} async-done(((bf16[512,512]{1,0:T(8,128)(2,1)}), bf16[2048,512]{1,0:T(8,128)(2,1)}) %all-gather.23.cloned.1.call-update) | async-done | bytes 2097168 | tf_op jit(solution)/shard_map/all_gather | solution.py:76
  59.5 3.3 convolution_convert_fusion.10
  67.3 16.4 all-gather.17.cloned.1.call-done
  83.7 2.3 fusion.81
  92.2 21.5 %all-gather.25.cloned.1.call-done = bf16[1024,512]{1,0:T(8,128)(2,1)} async-done(((bf16[256,512]{1,0:T(8,128)(2,1)}), bf16[1024,512]{1,0:T(8,128)(2,1)}) %all-gather.25.cloned.1.call-update) | async-done | bytes 1048592 | tf_op jit(solution)/shard_map/all_gather | solution.py:190
  113.7 2.1 reshape.295
  115.9 33.1 %all-gather.21.cloned.1.call-done = bf16[2048,1024]{1,0:T(8,128)(2,1)} async-done(((bf16[512,1024]{1,0:T(8,128)(2,1)}), bf16[2048,1024]{1,0:T(8,128)(2,1)}) %all-gather.21.cloned.1.call-update) | async-done | bytes 4194320 | tf_op jit(solution)/shard_map/all_gather | solution.py:76
  149.0 3.4 fusion.82
  155.1 25.9 %all-gather.19.cloned.1.call-done = bf16[1024,512]{0,1:T(8,128)(2,1)} async-done(((bf16[256,512]{0,1:T(8,128)(2,1)}), bf16[1024,512]{0,1:T(8,128)(2,1)}) %all-gather.19.cloned.1.call-update) | async-done | bytes 1048592 | tf_op jit(solution)/shard_map/all_gather | solution.py:189
  181.0 3.3 fusion.5
  188.0 3.3 fusion.54
  191.3 2.5 copy.56
  193.8 21.5 %all-gather.27.cloned.1.call-done = bf16[2048,1024]{1,0:T(8,128)(2,1)} async-done(((bf16[512,1024]{1,0:T(8,128)(2,1)}), bf16[2048,1024]{1,0:T(8,128)(2,1)}) %all-gather.27.cloned.1.call-update) | async-done | bytes 4194320 | tf_op jit(solution)/shard_map/all_gather | solution.py:76
  215.3 5.0 multiply_convert_fusion.7
  220.3 31.1 %all-gather.29.cloned.1.call-done = bf16[1024,2048]{1,0:T(8,128)(2,1)} async-done(((bf16[256,2048]{1,0:T(8,128)(2,1)}), bf16[1024,2048]{1,0:T(8,128)(2,1)}) %all-gather.29.cloned.1.call-update) | async-done | bytes 4194320 | tf_op jit(solution)/shard_map/all_gather | solution.py:76
  251.4 4.6 convolution_convert_fusion.8
  258.0 18.6 %reduce-scatter.10.cloned.1.call-done = bf16[128,2048]{1,0:T(8,128)(2,1)} async-done(((bf16[256,2048]{1,0:T(8,128)(2,1)}), bf16[128,2048]{1,0:T(8,128)(2,1)}) %reduce-scatter.10.cloned.1.call-update) | async-done | bytes 524304 | tf_op jit(solution)/shard_map/reduce_scatter | solution.py:69
  278.0 2.3 fusion.52
  283.6 18.2 %all-gather.31.cloned.1.call-done = bf16[256,2048]{1,0:T(8,128)(2,1)} async-done(((bf16[128,2048]{1,0:T(8,128)(2,1)}), bf16[256,2048]{1,0:T(8,128)(2,1)}) %all-gather.31.cloned.1.call-update) | async-done | bytes 1048592 | tf_op jit(solution)/shard_map/all_gather | solution.py:65
  301.8 83.7 %all-gather.33.cloned.1.call-done = bf16[2048,3072]{1,0:T(8,128)(2,1)} async-done(((bf16[512,3072]{1,0:T(8,128)(2,1)}), bf16[2048,3072]{1,0:T(8,128)(2,1)}) %all-gather.33.cloned.1.call-update) | async-done | bytes 12582928 | tf_op jit(solution)/shard_map/all_gather | solution.py:76
  385.5 10.0 fusion.83
  395.4 73.5 %all-gather.35.cloned.1.call-done = bf16[2048,3072]{1,0:T(8,128)(2,1)} async-done(((bf16[512,3072]{1,0:T(8,128)(2,1)}), bf16[2048,3072]{1,0:T(8,128)(2,1)}) %all-gather.35.cloned.1.call-update) | async-done | bytes 12582928 | tf_op jit(solution)/shard_map/all_gather | solution.py:76
  469.0 10.0 fusion.84
  479.0 13.4 all-gather.39.cloned.1.call-done
  492.4 83.6 %all-gather.37.cloned.1.call-done = bf16[3072,2048]{1,0:T(8,128)(2,1)} async-done(((bf16[768,2048]{1,0:T(8,128)(2,1)}), bf16[3072,2048]{1,0:T(8,128)(2,1)}) %all-gather.37.cloned.1.call-update) | async-done | bytes 12582928 | tf_op jit(solution)/shard_map/all_gather | solution.py:76
  576.0 13.4 multiply_convert_fusion
  589.3 7.1 fusion.85
  596.5 9.1 fusion.20
  605.7 20.5 %reduce-scatter.14.cloned.1.call-done = bf16[128,2048]{1,0:T(8,128)(2,1)} async-done(((bf16[256,2048]{1,0:T(8,128)(2,1)}), bf16[128,2048]{1,0:T(8,128)(2,1)}) %reduce-scatter.14.cloned.1.call-update) | async-done | bytes 524304 | tf_op jit(solution)/shard_map/reduce_scatter | solution.py:69
  626.2 2.2 fusion.43
  628.9 2.5 multiply_convert_fusion.5
  632.8 20.1 %all-gather.41.cloned.1.call-done = bf16[256,2048]{1,0:T(8,128)(2,1)} async-done(((bf16[128,2048]{1,0:T(8,128)(2,1)}), bf16[256,2048]{1,0:T(8,128)(2,1)}) %all-gather.41.cloned.1.call-update) | async-done | bytes 1048592 | tf_op jit(solution)/shard_map/all_gather | solution.py:65
  652.9 5.5 multiply_convert_fusion.4
  658.4 2.0 copy.57
  661.9 5.6 bitcast_convert_fusion
  667.5 5.6 fusion.2
  678.4 4.7 convolution_convert_fusion.3
  683.2 10.1 convolution_convert_fusion
  693.9 3.2 fusion.86
  698.2 2.4 copy.92
  700.6 2.4 copy.91
  708.2 3.3 convolution_convert_fusion.4
  711.5 3.3 convolution_convert_fusion.5
  714.9 7.3 reduce-scatter.16.cloned.1.call-done
  734.8 29.6 %pad_maximum_fusion.1 = bf16[2048,3072]{0,1:T(8,128)(2,1)} fusion(bf16[2048,1024]{0,1:T(8,128)(2,1)S(1)} %copy-done.3, bf16[2048,512]{0,1:T(8,128)(2,1)S(1)} %convolution_convert_fusion.6, bf16[2048,512]{0,1:T(8,128)(2,1)S(1)} %convolution_convert_fusion.7, bf16[2048,1024]{0,1:T(8,128)(2,1)S(1)} %copy-done.4), kind=kLoop, calls=%fused_computation.1 | loop fusion | flops 50331648 | bytes 25165824 | tf_op jit(solution)/shard_map/concatenate | solution.py:103
  765.6 8.0 convolution_convert_fusion.1
  773.6 8.4 convolution_convert_fusion.2
  782.0 20.1 %pad_maximum_fusion = bf16[2048,6144]{1,0:T(8,128)(2,1)} fusion(bf16[2048,3072]{1,0:T(8,128)(2,1)} %convolution_convert_fusion.1, bf16[2048,3072]{1,0:T(8,128)(2,1)} %convolution_convert_fusion.2), kind=kLoop, calls=%fused_computation | loop fusion | flops 50331648 | bytes 50331648 | tf_op jit(solution)/shard_map/concatenate | solution.py:103
  803.1 3.6 fusion.88
  811.9 9.7 convolution_convert_fusion.9
  821.7 49.5 %reduce-scatter.26.cloned.1.call-done = bf16[768,2048]{1,0:T(8,128)(2,1)} async-done(((bf16[3072,2048]{1,0:T(8,128)(2,1)}), bf16[768,2048]{1,0:T(8,128)(2,1)}) %reduce-scatter.26.cloned.1.call-update) | async-done | bytes 3145744 | tf_op jit(solution)/shard_map/reduce_scatter | solution.py:102
  871.2 99.6 %reduce-scatter.20.cloned.1.call-done = bf16[512,3072]{0,1:T(8,128)(2,1)} async-done(((bf16[2048,3072]{0,1:T(8,128)(2,1)}), bf16[512,3072]{0,1:T(8,128)(2,1)}) %reduce-scatter.20.cloned.1.call-update) | async-done | bytes 3145744 | tf_op jit(solution)/shard_map/reduce_scatter | solution.py:102
  970.8 184.5 %reduce-scatter.24.cloned.1.call-done = bf16[512,6144]{1,0:T(8,128)(2,1)} async-done(((bf16[2048,6144]{1,0:T(8,128)(2,1)}), bf16[512,6144]{1,0:T(8,128)(2,1)}) %reduce-scatter.24.cloned.1.call-update) | async-done | bytes 6291472 | tf_op jit(solution)/shard_map/reduce_scatter | solution.py:102
  1157.5 2.4 reshape.303
  1163.6 15.0 reduce-scatter.18.cloned.1.call-done
  1180.1 40.4 %all-reduce = (f32[2048]{0:T(1024)}, f32[128]{0:T(128)}, f32[128]{0:T(128)}, f32[2048]{0:T(1024)}) all-reduce(f32[2048]{0:T(1024)S(1)} %get-tuple-element.44, f32[128]{0:T(128)S(1)} %fusion.51, f32[128]{0:T(128)S(1)} %fusion.62, f32[2048]{0:T(1024)S(1)} %copy-done.46), channel_id=1, replica_groups=mesh['fsdp'=4,'ctx'=4,'tp'=2] {'fsdp','ctx','tp'}, use_global_device_ids=true, to_apply=%region_17.18 | all-reduce | flops 4352 | bytes 34816 | tf_op jit(solution)/shard_map/psum | solution.py:299
  1220.5 3.4 fusion.39
  1223.9 440.9 %all-reduce.4.cloned.1.call-done = (bf16[512,3072]{0,1:T(8,128)(2,1)}, bf16[512,6144]{1,0:T(8,128)(2,1)}, bf16[256,2048]{1,0:T(8,128)(2,1)}, bf16[768,2048]{1,0:T(8,128)(2,1)}) async-done(((bf16[512,3072]{0,1:T(8,128)(2,1)}, bf16[512,6144]{1,0:T(8,128)(2,1)}, bf16[256,2048]{1,0:T(8,128)(2,1)}, bf16[768,2048]{1,0:T(8,128)(2,1)}), (bf16[512,3072]{0,1:T(8,128)(2,1)}, bf16[512,6144]{1,0:T(8,128)(2,1)}, ...) | async-done | bytes 13631504 | tf_op jit(solution)/shard_map/psum | solution.py:119
  1664.8 4.3 fusion.76
  1669.4 2.9 copy.68
  1674.9 2.9 copy.71
  1679.3 9.4 fusion.75
  1688.7 3.5 convert_element_type.187
  (253 shorter events, 74.7 us)
Async XLA Ops:
  7.2 56.4 %copy-start.63 = (bf16[128]{0:T(256)(128)(2,1)S(1)}, bf16[128]{0:T(256)(128)(2,1)}, u32[]{:S(2)}) copy-start(bf16[128]{0:T(256)(128)(2,1)} %param.20) | copy-start | bytes 772
  7.2 56.4 %copy-start.59 = (s32[1,2]{1,0:T(1,128)S(1)}, s32[1,2]{1,0:T(1,128)}, u32[]{:S(2)}) copy-start(s32[1,2]{1,0:T(1,128)} %param.17) | copy-start | bytes 28
  7.2 28.2 %all-gather.15.cloned.1.call-start = ((), (), s32[]{:S(2)}) async-start(), calls=%async_computation.9 | async-start | bytes 1572864 | tf_op jit(solution)/shard_map/all_gather | solution.py:65
  7.9 4.8 copy-start.44
  11.2 48.3 %all-gather.23.cloned.1.call-start = ((), (), s32[]{:S(2)}) async-start(), calls=%async_computation.13 | async-start | bytes 2621440 | tf_op jit(solution)/shard_map/all_gather | solution.py:76
  12.0 71.7 %all-gather.17.cloned.1.call-start = ((), (), s32[]{:S(2)}) async-start(), calls=%async_computation.10 | async-start | bytes 2621440 | tf_op jit(solution)/shard_map/all_gather | solution.py:76
  12.7 101.0 %all-gather.25.cloned.1.call-start = ((), (), s32[]{:S(2)}) async-start(), calls=%async_computation.14 | async-start | bytes 1310720 | tf_op jit(solution)/shard_map/all_gather | solution.py:190
  35.4 48.3 %copy-start.2 = (bf16[256,2048]{1,0:T(8,128)(2,1)S(1)}, bf16[256,2048]{1,0:T(8,128)(2,1)}, u32[]{:S(2)}) copy-start(bf16[256,2048]{1,0:T(8,128)(2,1)} %all-gather.15.cloned.1.call-done) | copy-start | bytes 3145732
  62.9 86.1 %all-gather.21.cloned.1.call-start = ((), (), s32[]{:S(2)}) async-start(), calls=%async_computation.12 | async-start | bytes 5242880 | tf_op jit(solution)/shard_map/all_gather | solution.py:76
  63.5 117.5 %all-gather.19.cloned.1.call-start = ((), (), s32[]{:S(2)}) async-start(), calls=%async_computation.11 | async-start | bytes 1310720 | tf_op jit(solution)/shard_map/all_gather | solution.py:189
  63.6 23.4 %copy-start.54 = (f32[128]{0:T(128)}, f32[128]{0:T(128)S(1)}, u32[]{:S(2)}) copy-start(f32[128]{0:T(128)S(1)} %convert_element_type.150) | copy-start | bytes 1540
  67.3 87.1 %copy-start.27 = (f32[256,64]{1,0:T(8,128)}, f32[256,64]{1,0:T(8,128)S(1)}, u32[]{:S(2)}) copy-start(f32[256,64]{1,0:T(8,128)S(1)} %get-tuple-element.85) | copy-start | bytes 196612
  86.0 4.3 copy-start.23
  86.0 4.6 copy-start.64
  86.2 29.7 %copy-start.14 = (f32[256,4,128]{2,1,0:T(4,128)}, f32[256,4,128]{2,1,0:T(4,128)S(1)}, u32[]{:S(2)}) copy-start(f32[256,4,128]{2,1,0:T(4,128)S(1)} %reshape.292) | copy-start | bytes 1572868
  88.8 126.6 %all-gather.27.cloned.1.call-start = ((), (), s32[]{:S(2)}) async-start(), calls=%async_computation.15 | async-start | bytes 5242880 | tf_op jit(solution)/shard_map/all_gather | solution.py:76
  89.5 161.9 %all-gather.29.cloned.1.call-start = ((), (), s32[]{:S(2)}) async-start(), calls=%async_computation.16 | async-start | bytes 5242880 | tf_op jit(solution)/shard_map/all_gather | solution.py:76
  90.3 186.3 %reduce-scatter.10.cloned.1.call-start = ((), (), s32[]{:S(2)}) async-start(), calls=%async_computation.17 | async-start | bytes 1572864 | tf_op jit(solution)/shard_map/reduce_scatter | solution.py:69
  90.6 63.4 %copy-start.57 = (f32[128]{0:T(128)}, f32[128]{0:T(128)S(1)}, u32[]{:S(2)}) copy-start(f32[128]{0:T(128)S(1)} %convert_element_type.153) | copy-start | bytes 1540
  155.0 29.2 %copy-start.17 = (bf16[256,8,64]{2,0,1:T(8,128)(2,1)}, bf16[256,8,64]{2,0,1:T(8,128)(2,1)S(1)}, u32[]{:S(2)}) copy-start(bf16[256,8,64]{2,0,1:T(8,128)(2,1)S(1)} %copy.52) | copy-start | bytes 786436
  155.1 29.1 %copy-start.19 = (bf16[256,8,64]{2,0,1:T(8,128)(2,1)}, bf16[256,8,64]{2,0,1:T(8,128)(2,1)S(1)}, u32[]{:S(2)}) copy-start(bf16[256,8,64]{2,0,1:T(8,128)(2,1)S(1)} %copy.51) | copy-start | bytes 786436
  186.3 4.9 copy-start.47
  220.3 56.3 %copy-start.1 = (bf16[128,2048]{1,0:T(8,128)(2,1)S(1)}, bf16[128,2048]{1,0:T(8,128)(2,1)}, u32[]{:S(2)}) copy-start(bf16[128,2048]{1,0:T(8,128)(2,1)} %param.15) | copy-start | bytes 1572868
  251.4 26.6 %copy-start.24 = (bf16[128,2048]{1,0:T(8,128)(2,1)S(1)}, bf16[128,2048]{1,0:T(8,128)(2,1)}, u32[]{:S(2)}) copy-start(bf16[128,2048]{1,0:T(8,128)(2,1)} %param.16) | copy-start | bytes 1572868
  256.0 45.8 %all-gather.31.cloned.1.call-start = ((), (), s32[]{:S(2)}) async-start(), calls=%async_computation.18 | async-start | bytes 1572864 | tf_op jit(solution)/shard_map/all_gather | solution.py:65
  280.4 105.1 %all-gather.33.cloned.1.call-start = ((), (), s32[]{:S(2)}) async-start(), calls=%async_computation.19 | async-start | bytes 15728640 | tf_op jit(solution)/shard_map/all_gather | solution.py:76
  281.1 187.9 %all-gather.35.cloned.1.call-start = ((), (), s32[]{:S(2)}) async-start(), calls=%async_computation.20 | async-start | bytes 15728640 | tf_op jit(solution)/shard_map/all_gather | solution.py:76
  281.7 210.7 %all-gather.39.cloned.1.call-start = ((), (), s32[]{:S(2)}) async-start(), calls=%async_computation.23 | async-start | bytes 1572864 | tf_op jit(solution)/shard_map/all_gather | solution.py:65
  282.4 293.6 %all-gather.37.cloned.1.call-start = ((), (), s32[]{:S(2)}) async-start(), calls=%async_computation.21 | async-start | bytes 15728640 | tf_op jit(solution)/shard_map/all_gather | solution.py:76
  283.0 343.2 %reduce-scatter.14.cloned.1.call-start = ((), (), s32[]{:S(2)}) async-start(), calls=%async_computation.24 | async-start | bytes 1572864 | tf_op jit(solution)/shard_map/reduce_scatter | solution.py:69
  589.3 7.2 copy-start.38
  596.5 29.7 %copy-start.6 = (bf16[128,2048]{1,0:T(8,128)(2,1)S(1)}, bf16[128,2048]{1,0:T(8,128)(2,1)}, u32[]{:S(2)}) copy-start(bf16[128,2048]{1,0:T(8,128)(2,1)} %reduce-scatter.10.cloned.1.call-done) | copy-start | bytes 1572868
  605.6 47.3 %all-gather.41.cloned.1.call-start = ((), (), s32[]{:S(2)}) async-start(), calls=%async_computation.25 | async-start | bytes 1572864 | tf_op jit(solution)/shard_map/all_gather | solution.py:65
  631.5 90.7 %reduce-scatter.16.cloned.1.call-start = ((), (), s32[]{:S(2)}) async-start(), calls=%async_computation.26 | async-start | bytes 2621440 | tf_op jit(solution)/shard_map/reduce_scatter | solution.py:275
  652.9 9.0 copy-start.49
  661.9 5.6 copy-start.33
  661.9 5.6 copy-start.43
  667.5 7.6 copy-start.18
  667.5 7.6 copy-start.20
  678.4 143.3 %reduce-scatter.22.cloned.1.call-start = ((), (), s32[]{:S(2)}) async-start(), calls=%async_computation.29 | async-start | bytes 5242880 | tf_op jit(solution)/shard_map/reduce_scatter | solution.py:102
  683.1 188.0 %reduce-scatter.26.cloned.1.call-start = ((), (), s32[]{:S(2)}) async-start(), calls=%async_computation.31 | async-start | bytes 15728640 | tf_op jit(solution)/shard_map/reduce_scatter | solution.py:102
  693.3 277.5 %reduce-scatter.20.cloned.1.call-start = ((), (), s32[]{:S(2)}) async-start(), calls=%async_computation.28 | async-start | bytes 15728640 | tf_op jit(solution)/shard_map/reduce_scatter | solution.py:102
  697.2 5.8 copy-start.28
  698.2 6.6 copy-start.26
  714.9 13.5 copy-start.15
  714.9 13.5 copy-start.56
  726.8 4.7 copy-start.39
  730.0 4.8 copy-start.4
  764.4 390.9 %reduce-scatter.24.cloned.1.call-start = ((), (), s32[]{:S(2)}) async-start(), calls=%async_computation.30 | async-start | bytes 31457280 | tf_op jit(solution)/shard_map/reduce_scatter | solution.py:102
  765.6 8.0 copy-start.37
  802.1 4.6 copy-start.36
  802.1 376.5 %reduce-scatter.18.cloned.1.call-start = ((), (), s32[]{:S(2)}) async-start(), calls=%async_computation.27 | async-start | bytes 1572864 | tf_op jit(solution)/shard_map/reduce_scatter | solution.py:69
  811.8 408.6 %reduce-scatter.12.cloned.1.call-start = ((), (), s32[]{:S(2)}) async-start(), calls=%async_computation.22 | async-start | bytes 1572864 | tf_op jit(solution)/shard_map/reduce_scatter | solution.py:69
  821.6 843.2 %all-reduce.4.cloned.1.call-start = ((), (), s32[]{:S(2)}) async-start(), calls=%async_computation.32 | async-start | bytes 27262976 | tf_op jit(solution)/shard_map/psum | solution.py:119
  1155.3 4.7 copy-start.9
  1155.3 4.7 copy-start.11
  1155.4 23.2 %copy-start.45 = (f32[2048]{0:T(1024)S(1)}, f32[2048]{0:T(1024)}, u32[]{:S(2)}) copy-start(f32[2048]{0:T(1024)} %copy-done.44) | copy-start | bytes 24580
  1155.4 23.2 %copy-start.53 = (f32[128]{0:T(128)S(1)}, f32[128]{0:T(128)}, u32[]{:S(2)}) copy-start(f32[128]{0:T(128)} %copy-done.52) | copy-start | bytes 1540
  1157.4 22.7 %copy-start.46 = (f32[2048]{0:T(1024)S(1)}, f32[2048]{0:T(1024)}, u32[]{:S(2)}) copy-start(f32[2048]{0:T(1024)} %get-tuple-element.42) | copy-start | bytes 24580
  1157.4 63.1 %copy-start.48 = (f32[128]{0:T(128)S(1)}, f32[128]{0:T(128)}, u32[]{:S(2)}) copy-start(f32[128]{0:T(128)} %compare_convert_fusion) | copy-start | bytes 1540
  1157.4 63.1 %copy-start.51 = (f32[128]{0:T(128)S(1)}, f32[128]{0:T(128)}, u32[]{:S(2)}) copy-start(f32[128]{0:T(128)} %copy-done.50) | copy-start | bytes 1540
  1157.4 63.1 %copy-start.61 = (f32[128]{0:T(128)S(1)}, f32[128]{0:T(128)}, u32[]{:S(2)}) copy-start(f32[128]{0:T(128)} %copy-done.60) | copy-start | bytes 1540
  1664.8 4.3 copy-start.7
  1679.3 9.4 copy-start.29
  (25 other events, 56.9 us)
Sparse Core Ops, SparseCore 0:
  11.4 23.9 all-gather.14
  37.0 22.5 all-gather.22
  61.1 22.5 all-gather.16
  85.7 27.9 all-gather.24
  115.2 33.8 all-gather.20
  151.0 29.9 all-gather.18
  182.5 32.7 all-gather.26
  216.9 34.4 all-gather.28
  256.1 20.3 reduce-scatter.9
  280.5 21.2 all-gather.30
  303.4 82.0 all-gather.32
  386.9 82.0 all-gather.34
  471.1 21.2 all-gather.38
  493.8 82.1 all-gather.36
  605.7 20.3 reduce-scatter.13
  631.6 21.2 all-gather.40
  678.5 43.6 reduce-scatter.15
  725.1 43.7 reduce-scatter.21
  771.5 99.6 reduce-scatter.25
  873.6 97.1 reduce-scatter.19
  973.4 181.8 reduce-scatter.23
  1158.1 20.3 reduce-scatter.17
  1181.4 20.5 reduce-scatter.11
  1204.8 459.9 all-reduce.3
where the time goes:
time: 1700 us
  waiting for transfers between devices  1330 us (78%)
  matrix products  153 us (9%)
  other arithmetic  98.6 us (6%)
  local copies, waits for them, and re-layouts  58.1 us (3%)
  blocking collectives  40.4 us (2%)
    psum x1, waiting for transfers between devices, weight_grads(): summed = lax.psum(shared, 'ctx').astype(jnp.float32)  441 us
    all_gather x8, waiting for transfers between devices, fold_product(): lax.all_gather(a, 'fsdp', axis=0, tiled=True)  367 us
    reduce_scatter x4, waiting for transfers between devices, weight_grads(): lax.psum_scatter(jnp.concatenate([lax.dot_general(left_rows, grad_part, (...  334 us
    all_gather x4, waiting for transfers between devices, to_block(): return lax.all_gather(local_part, 'tp', axis=0, tiled=True)  74.3 us
    reduce_scatter x4, waiting for transfers between devices, to_share(): lax.psum_scatter(partial_rows.astype(jnp.bfloat16), 'tp', scatter_dimensi...  54.1 us
    concatenate x2, other arithmetic, weight_grads(): jnp.concatenate([lax.dot_general(left_rows, grad_part, (((0,), (0,)), (()...  49.7 us
    dot_general x8, matrix products, fold_product(): jnp.dot(left_rows, weight_part, preferred_element_type=jnp.float32)  48.3 us
    psum x1, blocking collectives, body(): lax.psum((gain_one_grad, query_gain_grad, key_gain_grad, gain_two_grad),...  40.4 us
  transfers between devices with their start and end apart: 24, of which 22 were waited for; matrix products, arithmetic and copies ran while one was open for 12% of the time, Pallas kernels for 0%

commit v1 on v0

--- a/solution.py
+++ b/solution.py
@@ -2,6 +2,7 @@
 import jax.numpy as jnp
 from jax import lax
 from jax.sharding import PartitionSpec as P
+from jax.lax import axis_index, ppermute, psum
 
 HEAD_SIZE = 128
 EPSILON = 1e-06
@@ -62,7 +63,21 @@
 
 
 def to_block(local_part):
-    return lax.all_gather(local_part, "tp", axis=0, tiled=True)
+
+    def samples_all_plan(local_array):
+        reached = psum(1, "tp")
+        moved = axis_index("tp")
+        piece_now, val2 = (reached, moved)
+        y2, f_now = (local_array, 1)
+        while f_now < piece_now:
+            ready = ppermute(y2, "tp", [(j0, j0 ^ f_now) for j0 in range(piece_now)])
+            item_now = jnp.concatenate([y2, ready], axis=0)
+            part_now = jnp.concatenate([ready, y2], axis=0)
+            y2 = jnp.where(val2 & f_now == 0, item_now, part_now)
+            f_now = 2 * f_now
+        return y2
+
+    return samples_all_plan(local_part)
 
 
 def to_share(partial_rows):

time: 1700 us -> 1620 us (0.953)
  waiting for transfers between devices: 1330 us -> 1250 us
    all_gather x4 -> x0, waiting for transfers between devices: 74.3 us -> none  [to_block(): return lax.all_gather(local_part, 'tp', axis=0, tiled=True)]
    all_gather x8, waiting for transfers between devices: 367 us -> 321 us  [fold_product(): lax.all_gather(a, 'fsdp', axis=0, tiled=True)]
    ppermute x0 -> x4, waiting for transfers between devices: none -> 37.3 us  [samples_all_plan(): ready = ppermute(y2, 'tp', [(j0, j0 ^ f_now) for j0 in range(piece_now)])]
  transfers between devices with their start and end apart: 24 -> 24, of which waited for: 22 -> 21; matrix products, arithmetic and copies ran while one was open for 12% -> 13% of each run, Pallas kernels for 0% -> 0%
where the time goes in v1:
time: 1620 us
  waiting for transfers between devices  1250 us (77%)
  matrix products  158 us (10%)
  other arithmetic  92.2 us (6%)
  local copies, waits for them, and re-layouts  55.5 us (3%)
  blocking collectives  40.4 us (2%)
  between operations  17.2 us (1%)
    psum x1, waiting for transfers between devices, weight_grads(): summed = lax.psum(shared, 'ctx').astype(jnp.float32)  441 us
    reduce_scatter x4, waiting for transfers between devices, weight_grads(): lax.psum_scatter(jnp.concatenate([lax.dot_general(left_rows, grad_part, (...  330 us
    all_gather x8, waiting for transfers between devices, fold_product(): lax.all_gather(a, 'fsdp', axis=0, tiled=True)  321 us
    reduce_scatter x4, waiting for transfers between devices, to_share(): lax.psum_scatter(partial_rows.astype(jnp.bfloat16), 'tp', scatter_dimensi...  53.1 us
    dot_general x8, matrix products, fold_product(): jnp.dot(left_rows, weight_part, preferred_element_type=jnp.float32)  48.3 us
    concatenate x2, other arithmetic, weight_grads(): jnp.concatenate([lax.dot_general(left_rows, grad_part, (((0,), (0,)), (()...  48 us
    dot_general x8, matrix products, weight_grads(): lax.dot_general(left_rows, grad_part, (((0,), (0,)), ((), ())), preferred...  44.6 us
    psum x1, blocking collectives, body(): lax.psum((gain_one_grad, query_gain_grad, key_gain_grad, gain_two_grad),...  40.4 us
  transfers between devices with their start and end apart: 24, of which 21 were waited for; matrix products, arithmetic and copies ran while one was open for 13% of the time, Pallas kernels for 0%

profile of v1, /device:TPU:0, one launch (start us, length us, event | category | flops | bytes accessed | tf_op | source)
XLA Modules:
  0.0 1615.5 jit_solution(14347022326201853339)
XLA Ops:
  11.9 3.1 collective-permute-start
  15.0 11.9 collective-permute-done
  26.9 8.0 all-gather.17.cloned.1.call-done
  34.9 3.0 convolution_convert_fusion.10
  42.3 16.8 %all-gather.11.cloned.1.call-done = bf16[2048,512]{1,0:T(8,128)(2,1)} async-done(((bf16[512,512]{1,0:T(8,128)(2,1)}), bf16[2048,512]{1,0:T(8,128)(2,1)}) %all-gather.11.cloned.1.call-update) | async-done | bytes 2097168 | tf_op jit(solution)/shard_map/all_gather | solution.py:91
  59.1 2.3 fusion.84
  67.7 21.6 %all-gather.19.cloned.1.call-done = bf16[1024,512]{1,0:T(8,128)(2,1)} async-done(((bf16[256,512]{1,0:T(8,128)(2,1)}), bf16[1024,512]{1,0:T(8,128)(2,1)}) %all-gather.19.cloned.1.call-update) | async-done | bytes 1048592 | tf_op jit(solution)/shard_map/all_gather | solution.py:205
  89.3 2.1 reshape.295
  91.5 33.1 %all-gather.15.cloned.1.call-done = bf16[2048,1024]{1,0:T(8,128)(2,1)} async-done(((bf16[512,1024]{1,0:T(8,128)(2,1)}), bf16[2048,1024]{1,0:T(8,128)(2,1)}) %all-gather.15.cloned.1.call-update) | async-done | bytes 4194320 | tf_op jit(solution)/shard_map/all_gather | solution.py:91
  124.6 3.8 fusion.83
  130.0 26.5 %all-gather.13.cloned.1.call-done = bf16[1024,512]{0,1:T(8,128)(2,1)} async-done(((bf16[256,512]{0,1:T(8,128)(2,1)}), bf16[1024,512]{0,1:T(8,128)(2,1)}) %all-gather.13.cloned.1.call-update) | async-done | bytes 1048592 | tf_op jit(solution)/shard_map/all_gather | solution.py:204
  156.5 3.3 fusion.5
  159.8 2.0 fusion.7
  163.6 3.3 fusion.54
  166.8 2.5 copy.56
  169.4 21.4 %all-gather.21.cloned.1.call-done = bf16[2048,1024]{1,0:T(8,128)(2,1)} async-done(((bf16[512,1024]{1,0:T(8,128)(2,1)}), bf16[2048,1024]{1,0:T(8,128)(2,1)}) %all-gather.21.cloned.1.call-update) | async-done | bytes 4194320 | tf_op jit(solution)/shard_map/all_gather | solution.py:91
  190.7 5.1 multiply_convert_fusion.7
  195.8 30.9 %all-gather.23.cloned.1.call-done = bf16[1024,2048]{1,0:T(8,128)(2,1)} async-done(((bf16[256,2048]{1,0:T(8,128)(2,1)}), bf16[1024,2048]{1,0:T(8,128)(2,1)}) %all-gather.23.cloned.1.call-update) | async-done | bytes 4194320 | tf_op jit(solution)/shard_map/all_gather | solution.py:91
  226.8 4.4 convolution_convert_fusion.8
  235.4 16.4 %reduce-scatter.10.cloned.1.call-done = bf16[128,2048]{1,0:T(8,128)(2,1)} async-done(((bf16[256,2048]{1,0:T(8,128)(2,1)}), bf16[128,2048]{1,0:T(8,128)(2,1)}) %reduce-scatter.10.cloned.1.call-update) | async-done | bytes 524304 | tf_op jit(solution)/shard_map/reduce_scatter | solution.py:84
  253.2 2.3 fusion.52
  258.3 12.9 collective-permute-done.1
  271.2 64.3 %all-gather.25.cloned.1.call-done = bf16[2048,3072]{1,0:T(8,128)(2,1)} async-done(((bf16[512,3072]{1,0:T(8,128)(2,1)}), bf16[2048,3072]{1,0:T(8,128)(2,1)}) %all-gather.25.cloned.1.call-update) | async-done | bytes 12582928 | tf_op jit(solution)/shard_map/all_gather | solution.py:91
  335.4 10.3 fusion.82
  345.7 73.2 %all-gather.27.cloned.1.call-done = bf16[2048,3072]{1,0:T(8,128)(2,1)} async-done(((bf16[512,3072]{1,0:T(8,128)(2,1)}), bf16[2048,3072]{1,0:T(8,128)(2,1)}) %all-gather.27.cloned.1.call-update) | async-done | bytes 12582928 | tf_op jit(solution)/shard_map/all_gather | solution.py:91
  418.9 10.0 fusion.81
  428.9 73.7 %all-gather.29.cloned.1.call-done = bf16[3072,2048]{1,0:T(8,128)(2,1)} async-done(((bf16[768,2048]{1,0:T(8,128)(2,1)}), bf16[3072,2048]{1,0:T(8,128)(2,1)}) %all-gather.29.cloned.1.call-update) | async-done | bytes 12582928 | tf_op jit(solution)/shard_map/all_gather | solution.py:91
  502.6 13.8 multiply_convert_fusion
  516.4 7.2 fusion.91
  523.6 9.1 fusion.20
  532.8 20.5 %reduce-scatter.14.cloned.1.call-done = bf16[128,2048]{1,0:T(8,128)(2,1)} async-done(((bf16[256,2048]{1,0:T(8,128)(2,1)}), bf16[128,2048]{1,0:T(8,128)(2,1)}) %reduce-scatter.14.cloned.1.call-update) | async-done | bytes 524304 | tf_op jit(solution)/shard_map/reduce_scatter | solution.py:84
  553.3 2.3 fusion.43
  558.4 12.5 collective-permute-done.3
  571.0 4.8 multiply_convert_fusion.4
  575.8 2.0 copy.57
  579.4 5.6 bitcast_convert_fusion
  585.0 5.7 fusion.2
  594.4 4.4 convolution_convert_fusion.3
  598.8 10.4 convolution_convert_fusion
  610.5 2.9 fusion.92
  619.9 3.3 convolution_convert_fusion.4
  625.6 3.3 convolution_convert_fusion.5
  628.9 9.2 reduce-scatter.16.cloned.1.call-done
  649.3 2.1 copy-done.22
  651.4 29.4 %pad_maximum_fusion.1 = bf16[2048,3072]{0,1:T(8,128)(2,1)} fusion(bf16[2048,1024]{0,1:T(8,128)(2,1)S(1)} %copy-done.22, bf16[2048,512]{0,1:T(8,128)(2,1)S(1)} %convolution_convert_fusion.6, bf16[2048,512]{0,1:T(8,128)(2,1)S(1)} %convolution_convert_fusion.7, bf16[2048,1024]{0,1:T(8,128)(2,1)S(1)} %copy-done.23), kind=kLoop, calls=%fused_computation.1 | loop fusion | flops 50331648 | bytes 25165824 | tf_op jit(solution)/shard_map/concatenate | solution.py:118
  681.8 9.9 convolution_convert_fusion.1
  691.8 11.6 convolution_convert_fusion.2
  703.4 18.6 %pad_maximum_fusion = bf16[2048,6144]{1,0:T(8,128)(2,1)} fusion(bf16[2048,3072]{1,0:T(8,128)(2,1)} %convolution_convert_fusion.1, bf16[2048,3072]{1,0:T(8,128)(2,1)} %convolution_convert_fusion.2), kind=kLoop, calls=%fused_computation | loop fusion | flops 50331648 | bytes 50331648 | tf_op jit(solution)/shard_map/concatenate | solution.py:118
  722.3 3.8 fusion.94
  731.4 9.4 convolution_convert_fusion.9
  741.0 46.0 %reduce-scatter.26.cloned.1.call-done = bf16[768,2048]{1,0:T(8,128)(2,1)} async-done(((bf16[3072,2048]{1,0:T(8,128)(2,1)}), bf16[768,2048]{1,0:T(8,128)(2,1)}) %reduce-scatter.26.cloned.1.call-update) | async-done | bytes 3145744 | tf_op jit(solution)/shard_map/reduce_scatter | solution.py:117
  786.9 99.6 %reduce-scatter.20.cloned.1.call-done = bf16[512,3072]{0,1:T(8,128)(2,1)} async-done(((bf16[2048,3072]{0,1:T(8,128)(2,1)}), bf16[512,3072]{0,1:T(8,128)(2,1)}) %reduce-scatter.20.cloned.1.call-update) | async-done | bytes 3145744 | tf_op jit(solution)/shard_map/reduce_scatter | solution.py:117
  886.5 184.4 %reduce-scatter.24.cloned.1.call-done = bf16[512,6144]{1,0:T(8,128)(2,1)} async-done(((bf16[2048,6144]{1,0:T(8,128)(2,1)}), bf16[512,6144]{1,0:T(8,128)(2,1)}) %reduce-scatter.24.cloned.1.call-update) | async-done | bytes 6291472 | tf_op jit(solution)/shard_map/reduce_scatter | solution.py:117
  1073.0 2.4 reshape.303
  1075.6 2.0 fusion.51
  1077.9 16.1 reduce-scatter.18.cloned.1.call-done
  1095.5 40.4 %all-reduce = (f32[2048]{0:T(1024)}, f32[128]{0:T(128)}, f32[128]{0:T(128)}, f32[2048]{0:T(1024)}) all-reduce(f32[2048]{0:T(1024)S(1)} %get-tuple-element.44, f32[128]{0:T(128)S(1)} %fusion.51, f32[128]{0:T(128)S(1)} %fusion.62, f32[2048]{0:T(1024)S(1)} %copy-done.53), channel_id=1, replica_groups=mesh['fsdp'=4,'ctx'=4,'tp'=2] {'fsdp','ctx','tp'}, use_global_device_ids=true, to_apply=%region_17.18 | all-reduce | flops 4352 | bytes 34816 | tf_op jit(solution)/shard_map/psum | solution.py:314
  1136.0 3.4 fusion.39
  1139.4 440.9 %all-reduce.4.cloned.1.call-done = (bf16[512,3072]{0,1:T(8,128)(2,1)}, bf16[512,6144]{1,0:T(8,128)(2,1)}, bf16[256,2048]{1,0:T(8,128)(2,1)}, bf16[768,2048]{1,0:T(8,128)(2,1)}) async-done(((bf16[512,3072]{0,1:T(8,128)(2,1)}, bf16[512,6144]{1,0:T(8,128)(2,1)}, bf16[256,2048]{1,0:T(8,128)(2,1)}, bf16[768,2048]{1,0:T(8,128)(2,1)}), (bf16[512,3072]{0,1:T(8,128)(2,1)}, bf16[512,6144]{1,0:T(8,128)(2,1)}, ...) | async-done | bytes 13631504 | tf_op jit(solution)/shard_map/psum | solution.py:134
  1580.2 3.6 fusion.86
  1585.1 2.9 copy.68
  1588.0 2.5 copy.69
  1595.2 9.4 fusion.85
  1604.6 3.5 convert_element_type.187
  (281 shorter events, 71.3 us)
Async XLA Ops:
  7.2 27.7 %all-gather.17.cloned.1.call-start = ((), (), s32[]{:S(2)}) async-start(), calls=%async_computation.12 | async-start | bytes 2621440 | tf_op jit(solution)/shard_map/all_gather | solution.py:91
  7.9 51.2 %all-gather.11.cloned.1.call-start = ((), (), s32[]{:S(2)}) async-start(), calls=%async_computation.9 | async-start | bytes 2621440 | tf_op jit(solution)/shard_map/all_gather | solution.py:91
  8.7 80.7 %all-gather.19.cloned.1.call-start = ((), (), s32[]{:S(2)}) async-start(), calls=%async_computation.13 | async-start | bytes 1310720 | tf_op jit(solution)/shard_map/all_gather | solution.py:205
  11.9 112.7 %copy-start.41 = (bf16[128,2048]{1,0:T(8,128)(2,1)}, bf16[128,2048]{1,0:T(8,128)(2,1)S(1)}, u32[]{:S(2)}) copy-start(bf16[128,2048]{1,0:T(8,128)(2,1)S(1)} %fusion.44) | copy-start | bytes 1572868
  11.9 15.0 collective-permute-start
  15.0 23.5 %copy-start.76 = (bf16[128]{0:T(256)(128)(2,1)S(1)}, bf16[128]{0:T(256)(128)(2,1)}, u32[]{:S(2)}) copy-start(bf16[128]{0:T(256)(128)(2,1)} %param.20) | copy-start | bytes 772
  15.0 23.6 %copy-start.67 = (s32[1,2]{1,0:T(1,128)S(1)}, s32[1,2]{1,0:T(1,128)}, u32[]{:S(2)}) copy-start(s32[1,2]{1,0:T(1,128)} %param.17) | copy-start | bytes 28
  26.9 32.2 %copy-start.71 = (bf16[128,2048]{1,0:T(8,128)(2,1)}, bf16[128,2048]{1,0:T(8,128)(2,1)S(1)}, u32[]{:S(2)}) copy-start(bf16[128,2048]{1,0:T(8,128)(2,1)S(1)} %collective-permute-done) | copy-start | bytes 1572868
  37.9 86.7 %all-gather.15.cloned.1.call-start = ((), (), s32[]{:S(2)}) async-start(), calls=%async_computation.11 | async-start | bytes 5242880 | tf_op jit(solution)/shard_map/all_gather | solution.py:91
  38.5 118.0 %all-gather.13.cloned.1.call-start = ((), (), s32[]{:S(2)}) async-start(), calls=%async_computation.10 | async-start | bytes 1310720 | tf_op jit(solution)/shard_map/all_gather | solution.py:204
  38.6 23.5 %copy-start.62 = (f32[128]{0:T(128)}, f32[128]{0:T(128)S(1)}, u32[]{:S(2)}) copy-start(f32[128]{0:T(128)S(1)} %convert_element_type.150) | copy-start | bytes 1540
  42.3 87.0 %copy-start.26 = (f32[256,64]{1,0:T(8,128)}, f32[256,64]{1,0:T(8,128)S(1)}, u32[]{:S(2)}) copy-start(f32[256,64]{1,0:T(8,128)S(1)} %get-tuple-element.85) | copy-start | bytes 196612
  62.0 4.1 copy-start.77
  64.2 126.5 %all-gather.21.cloned.1.call-start = ((), (), s32[]{:S(2)}) async-start(), calls=%async_computation.14 | async-start | bytes 5242880 | tf_op jit(solution)/shard_map/all_gather | solution.py:91
  64.8 162.0 %all-gather.23.cloned.1.call-start = ((), (), s32[]{:S(2)}) async-start(), calls=%async_computation.15 | async-start | bytes 5242880 | tf_op jit(solution)/shard_map/all_gather | solution.py:91
  65.5 186.3 %reduce-scatter.10.cloned.1.call-start = ((), (), s32[]{:S(2)}) async-start(), calls=%async_computation.16 | async-start | bytes 1572864 | tf_op jit(solution)/shard_map/reduce_scatter | solution.py:84
  66.1 62.8 %copy-start.65 = (f32[128]{0:T(128)}, f32[128]{0:T(128)S(1)}, u32[]{:S(2)}) copy-start(f32[128]{0:T(128)S(1)} %convert_element_type.153) | copy-start | bytes 1540
  159.8 3.8 copy-start
  161.8 5.0 copy-start.54
  163.6 27.1 %copy-start.42 = (bf16[128,2048]{1,0:T(8,128)(2,1)S(1)}, bf16[128,2048]{1,0:T(8,128)(2,1)}, u32[]{:S(2)}) copy-start(bf16[128,2048]{1,0:T(8,128)(2,1)} %copy-done.41) | copy-start | bytes 1572868
  195.8 35.3 %copy-start.79 = (bf16[256,1024]{1,0:T(8,128)(2,1)}, bf16[256,1024]{1,0:T(8,128)(2,1)S(1)}, u32[]{:S(2)}) copy-start(bf16[256,1024]{1,0:T(8,128)(2,1)S(1)} %get-tuple-element.92) | copy-start | bytes 1572868
  231.2 104.2 %all-gather.25.cloned.1.call-start = ((), (), s32[]{:S(2)}) async-start(), calls=%async_computation.17 | async-start | bytes 15728640 | tf_op jit(solution)/shard_map/all_gather | solution.py:91
  231.9 19.8 %copy-start.1 = (bf16[128,2048]{1,0:T(8,128)(2,1)S(1)}, bf16[128,2048]{1,0:T(8,128)(2,1)}, u32[]{:S(2)}) copy-start(bf16[128,2048]{1,0:T(8,128)(2,1)} %param.15) | copy-start | bytes 1572868
  232.0 21.2 %copy-start.18 = (bf16[128,2048]{1,0:T(8,128)(2,1)S(1)}, bf16[128,2048]{1,0:T(8,128)(2,1)}, u32[]{:S(2)}) copy-start(bf16[128,2048]{1,0:T(8,128)(2,1)} %param.16) | copy-start | bytes 1572868
  232.0 187.0 %all-gather.27.cloned.1.call-start = ((), (), s32[]{:S(2)}) async-start(), calls=%async_computation.18 | async-start | bytes 15728640 | tf_op jit(solution)/shard_map/all_gather | solution.py:91
  232.6 270.1 %all-gather.29.cloned.1.call-start = ((), (), s32[]{:S(2)}) async-start(), calls=%async_computation.19 | async-start | bytes 15728640 | tf_op jit(solution)/shard_map/all_gather | solution.py:91
  233.3 320.0 %reduce-scatter.14.cloned.1.call-start = ((), (), s32[]{:S(2)}) async-start(), calls=%async_computation.21 | async-start | bytes 1572864 | tf_op jit(solution)/shard_map/reduce_scatter | solution.py:84
  256.3 14.9 collective-permute-start.1
  256.6 162.4 %copy-start.20 = (bf16[128,2048]{1,0:T(8,128)(2,1)S(1)}, bf16[128,2048]{1,0:T(8,128)(2,1)}, u32[]{:S(2)}) copy-start(bf16[128,2048]{1,0:T(8,128)(2,1)} %copy-done.19) | copy-start | bytes 1572868
  256.6 172.3 %collective-permute-start.2 = (bf16[128,2048]{1,0:T(8,128)(2,1)}, bf16[128,2048]{1,0:T(8,128)(2,1)}, u32[]{:S(2)}, u32[]{:S(2)}) collective-permute-start(bf16[128,2048]{1,0:T(8,128)(2,1)} %get-tuple-element.86), channel_id=1, source_target_pairs={{0,1},{1,0},{2,3},{3,2},{4,5},{5,4},{6,7},{7,6},{8,9},{9,8},{10,11... | collective-permute-start | bytes 1572872 | tf_op jit(solution)/shard_map/ppermute | solution.py:73
  516.4 7.2 copy-start.34
  523.6 29.7 %copy-start.3 = (bf16[128,2048]{1,0:T(8,128)(2,1)S(1)}, bf16[128,2048]{1,0:T(8,128)(2,1)}, u32[]{:S(2)}) copy-start(bf16[128,2048]{1,0:T(8,128)(2,1)} %reduce-scatter.10.cloned.1.call-done) | copy-start | bytes 1572868
  532.7 105.3 %reduce-scatter.16.cloned.1.call-start = ((), (), s32[]{:S(2)}) async-start(), calls=%async_computation.22 | async-start | bytes 2621440 | tf_op jit(solution)/shard_map/reduce_scatter | solution.py:290
  553.3 4.5 copy-start.55
  553.3 17.7 %copy-start.38 = (f32[256,1024]{1,0:T(8,128)S(1)}, f32[256,1024]{1,0:T(8,128)}, u32[]{:S(2)}) copy-start(f32[256,1024]{1,0:T(8,128)} %copy.56) | copy-start | bytes 3145732
  553.3 17.7 %copy-start.80 = (f32[256,1024]{1,0:T(8,128)S(1)}, f32[256,1024]{1,0:T(8,128)}, u32[]{:S(2)}) copy-start(f32[256,1024]{1,0:T(8,128)} %get-tuple-element.93) | copy-start | bytes 3145732
  555.6 15.3 copy-start.68
  557.4 18.4 %copy-start.45 = (bf16[128,2048]{1,0:T(8,128)(2,1)}, bf16[128,2048]{1,0:T(8,128)(2,1)S(1)}, u32[]{:S(2)}) copy-start(bf16[128,2048]{1,0:T(8,128)(2,1)S(1)} %multiply_convert_fusion.5) | copy-start | bytes 1572868
  557.4 13.6 collective-permute-start.3
  571.0 4.8 copy-start.74
  571.0 8.4 copy-start.57
  579.4 5.6 copy-start.30
  579.4 5.6 copy-start.37
  594.3 146.6 %reduce-scatter.22.cloned.1.call-start = ((), (), s32[]{:S(2)}) async-start(), calls=%async_computation.25 | async-start | bytes 5242880 | tf_op jit(solution)/shard_map/reduce_scatter | solution.py:117
  598.8 188.2 %reduce-scatter.26.cloned.1.call-start = ((), (), s32[]{:S(2)}) async-start(), calls=%async_computation.27 | async-start | bytes 15728640 | tf_op jit(solution)/shard_map/reduce_scatter | solution.py:117
  609.2 277.3 %reduce-scatter.20.cloned.1.call-start = ((), (), s32[]{:S(2)}) async-start(), calls=%async_computation.24 | async-start | bytes 15728640 | tf_op jit(solution)/shard_map/reduce_scatter | solution.py:117
  619.8 4.0 copy-start.8
  628.9 15.5 copy-start.10
  628.9 15.5 copy-start.64
  680.8 390.1 %reduce-scatter.24.cloned.1.call-start = ((), (), s32[]{:S(2)}) async-start(), calls=%async_computation.26 | async-start | bytes 31457280 | tf_op jit(solution)/shard_map/reduce_scatter | solution.py:117
  681.8 9.9 copy-start.33
  722.0 4.1 copy-start.48
  722.0 372.0 %reduce-scatter.18.cloned.1.call-start = ((), (), s32[]{:S(2)}) async-start(), calls=%async_computation.23 | async-start | bytes 1572864 | tf_op jit(solution)/shard_map/reduce_scatter | solution.py:84
  722.3 3.8 copy-start.70
  731.4 404.6 %reduce-scatter.12.cloned.1.call-start = ((), (), s32[]{:S(2)}) async-start(), calls=%async_computation.20 | async-start | bytes 1572864 | tf_op jit(solution)/shard_map/reduce_scatter | solution.py:84
  740.9 839.3 %all-reduce.4.cloned.1.call-start = ((), (), s32[]{:S(2)}) async-start(), calls=%async_computation.28 | async-start | bytes 27262976 | tf_op jit(solution)/shard_map/psum | solution.py:134
  1070.9 4.6 copy-start.6
  1073.0 21.0 %copy-start.52 = (f32[2048]{0:T(1024)S(1)}, f32[2048]{0:T(1024)}, u32[]{:S(2)}) copy-start(f32[2048]{0:T(1024)} %copy-done.51) | copy-start | bytes 24580
  1073.0 21.0 %copy-start.61 = (f32[128]{0:T(128)S(1)}, f32[128]{0:T(128)}, u32[]{:S(2)}) copy-start(f32[128]{0:T(128)} %copy-done.60) | copy-start | bytes 1540
  1075.4 20.1 %copy-start.53 = (f32[2048]{0:T(1024)S(1)}, f32[2048]{0:T(1024)}, u32[]{:S(2)}) copy-start(f32[2048]{0:T(1024)} %get-tuple-element.42) | copy-start | bytes 24580
  1075.4 60.5 %copy-start.56 = (f32[128]{0:T(128)S(1)}, f32[128]{0:T(128)}, u32[]{:S(2)}) copy-start(f32[128]{0:T(128)} %compare_convert_fusion) | copy-start | bytes 1540
  1075.4 60.5 %copy-start.59 = (f32[128]{0:T(128)S(1)}, f32[128]{0:T(128)}, u32[]{:S(2)}) copy-start(f32[128]{0:T(128)} %copy-done.58) | copy-start | bytes 1540
  1075.4 60.5 %copy-start.69 = (f32[128]{0:T(128)S(1)}, f32[128]{0:T(128)}, u32[]{:S(2)}) copy-start(f32[128]{0:T(128)} %copy-done.68) | copy-start | bytes 1540
  1595.2 9.4 copy-start.28
  (41 other events, 79.4 us)
Sparse Core Ops, SparseCore 0:
  9.5 25.2 all-gather.16
  36.4 22.6 all-gather.10
  61.3 28.0 all-gather.18
  90.7 33.7 all-gather.14
  126.5 29.9 all-gather.12
  157.9 32.7 all-gather.20
  192.3 34.4 all-gather.22
  231.3 20.3 reduce-scatter.9
  253.3 82.0 all-gather.24
  336.8 82.0 all-gather.26
  420.5 82.0 all-gather.28
  532.8 20.3 reduce-scatter.13
  594.4 43.5 reduce-scatter.15
  641.0 43.7 reduce-scatter.21
  687.3 99.6 reduce-scatter.25
  789.4 97.1 reduce-scatter.19
  889.0 181.8 reduce-scatter.23
  1073.6 20.3 reduce-scatter.17
  1096.8 20.6 reduce-scatter.11
  1120.3 459.8 all-reduce.3
